TPU v7x, 128 devices: a whole 4x4x4 slice. The times are simulated.
128 devices in a mesh: seq: 64 (over x_lo, z, y, core), head: 2 (over x_hi).
Axes of the slice: x: 4 (x_hi: 2, x_lo: 2; x = x_hi * 2 + x_lo), y: 4, z: 4, core: 2. Of those that a mesh axis runs over, the one named last changes fastest.
Arguments:
- query_tensor: float32 [32768, 32, 128], P('seq', 'head'), may hold values from -6 to 6
- key_tensor: float32 [32768, 16, 128], P('seq', 'head'), may hold values from -6 to 6
- value_tensor: float32 [32768, 16, 128], P('seq', 'head'), may hold values from -6 to 6
- output_gradient: float32 [32768, 32, 128], P('seq', 'head'), may hold values from -24 to 24
- logsumexp: float32 [32, 32768], P('head', 'seq'), may hold values from 5.5 to 7
- row_inner_products: float32 [32, 32768], P('head', 'seq'), may hold values from -120 to 120
Outputs:
- query_grad: float32 [32768, 32, 128], P('seq', 'head')
- key_grad: float32 [32768, 16, 128], P('seq', 'head')
- value_grad: float32 [32768, 16, 128], P('seq', 'head')
All inputs are finite; a program needn't handle non-finite values.
Results may differ from a plain program's by a relative error of at most 0.0053.
Values may be sent and summed in bfloat16 or wider, within the bound.
No kernel may reach another device: no remote copies, remote signals or barrier semaphores. Data moves between devices by JAX's collectives and lax.ppermute only.
A program may use at most 192 MiB of HBM per device.

v0:
```python
import math

import jax
import jax.numpy as jnp
from jax import lax
from jax.experimental import pallas as pl
from jax.experimental.pallas import tpu as pltpu
from jax.sharding import PartitionSpec as P


QSCALE = 168
SCALE = QSCALE ** (-0.5)
LOG2E = math.log2(math.e)
VMEM = 24 * 1024 * 1024
GROUPS = (1, 1, 1, 1)
MINE = 4
F32, BF16 = jnp.float32, jnp.bfloat16
NT = (((1,), (1,)), ((), ()))
NN = (((1,), (0,)), ((), ()))
HBM = pl.BlockSpec(memory_space=pl.ANY)
GIVEN = pl.BlockSpec(memory_space=pltpu.HBM)
SCALAR = pl.BlockSpec(memory_space=pltpu.SMEM)
PARAMS = pltpu.CompilerParams(vmem_limit_bytes=VMEM)
ALONE = pltpu.CompilerParams(vmem_limit_bytes=64 * 1000 * 1024)


def dot(a, b, dims):
    return lax.dot_general(a, b, dims, preferred_element_type=F32)


def rotated(x, by):
    count = lax.axis_size("seq")
    return lax.ppermute(x, "seq", [(i, (i + by) % count) for i in range(count)])


def crossed(x, by):
    count = lax.axis_size("seq")
    return lax.ppermute(x, "seq", [(i, ((i + by) % count) ^ 1) for i in range(count)])


def partner(x):
    count = lax.axis_size("seq")
    return lax.ppermute(x, "seq", [(i, i ^ 1) for i in range(count)])


def cost(nbytes, flops=0, exps=0):
    return pl.CostEstimate(flops=flops, transcendentals=exps, bytes_accessed=nbytes)


def like(shape, dtype):
    return jax.ShapeDtypeStruct(shape, dtype)


def pack_kv(place, keys, values, lse, dots):
    tokens, heads, _, width = keys.shape

    def body(place_ref, k, v, lse_ref, dots_ref, *rest):
        keep, *parts, give, rows = rest[: 3 + 2 * len(GROUPS)]
        wide, narrow, rows_buf, in_sem, out_sem, part_sem, row_sem = rest[3 + 2 * len(GROUPS) :]
        spots = [(c, x) for c, n in enumerate(GROUPS) for x in range(n)]
        core = lax.rem(place_ref[0], 2)
        order = [(part, i) for part in range(2) for i in range(MINE)]

        def load(n, t):
            part, i = order[n]
            half = 1 - core if part == 0 else core
            return pltpu.make_async_copy((k, v)[t].at[:, half * MINE + i, 0, :], wide.at[n, t], in_sem.at[n, t])

        for n in range(len(order)):
            for t in range(2):
                load(n, t).start()
        row_loads = [pltpu.make_async_copy(x, rows_buf.at[t], row_sem.at[t]) for t, x in enumerate((lse_ref, dots_ref))]
        for c in row_loads:
            c.start()
        for c in row_loads:
            c.wait()
        waits = [pltpu.make_async_copy(rows_buf, rows, row_sem.at[2])]
        waits[0].start()
        for n, (part, i) in enumerate(order):
            for t in range(2):
                load(n, t).wait()
                narrow[n, t] = wide[n, t].astype(BF16)
            c, x = spots[i]
            target = parts[c if part else len(GROUPS) + c].at[x]
            waits.append(pltpu.make_async_copy(narrow.at[n], target, part_sem.at[n]))
            waits[-1].start()
            waits.append(pltpu.make_async_copy(narrow.at[n], (give, keep)[part].at[i], out_sem.at[n]))
            waits[-1].start()
        for w in waits:
            w.wait()

    return pl.pallas_call(
        body,
        in_specs=[SCALAR] + [GIVEN] * 4,
        out_specs=[HBM] * (3 + 2 * len(GROUPS)),
        out_shape=[
            like((MINE, 2, tokens, width), BF16),
            *[like((n, 2, tokens, width), BF16) for n in GROUPS] * 2,
            like((MINE, 2, tokens, width), BF16),
            like((2, *lse.shape), F32),
        ],
        scratch_shapes=[
            pltpu.VMEM((2 * MINE, 2, tokens, width), F32),
            pltpu.VMEM((2 * MINE, 2, tokens, width), BF16),
            pltpu.VMEM((2, *lse.shape), F32),
            pltpu.SemaphoreType.DMA((2 * MINE, 2)),
            pltpu.SemaphoreType.DMA((2 * MINE,)),
            pltpu.SemaphoreType.DMA((2 * MINE,)),
            pltpu.SemaphoreType.DMA((3,)),
        ],
        compiler_params=ALONE,
        cost_estimate=cost(tokens * heads * width * 12),
        name="pack_kv",
    )(place, keys, values, lse, dots)


def pack_qg(give, place, queries, gradients):
    tokens, _, _, width = queries.shape

    def body(place_ref, q, g, out, wide, narrow, in_sem, out_sem):
        core = lax.rem(place_ref[0], 2)
        half = 1 - core if give else core
        order = [(i, j, t) for i in range(MINE) for j in range(2) for t in range(2)]

        def load(i, j, t):
            return pltpu.make_async_copy(
                (q, g)[t].at[:, 2 * (half * MINE + i) + j, 0, :], wide.at[i, j, t], in_sem.at[i, j, t]
            )

        for o in order:
            load(*o).start()
        waits = []
        for i in range(MINE):
            for j in range(2):
                for t in range(2):
                    load(i, j, t).wait()
                    narrow[i, j, t] = wide[i, j, t].astype(BF16)
            waits.append(pltpu.make_async_copy(narrow.at[i], out.at[i], out_sem.at[i]))
            waits[-1].start()
        for w in waits:
            w.wait()

    shape = (MINE, 2, 2, tokens, width)
    return pl.pallas_call(
        body,
        in_specs=[SCALAR, GIVEN, GIVEN],
        out_specs=HBM,
        out_shape=like(shape, BF16),
        scratch_shapes=[
            pltpu.VMEM(shape, F32),
            pltpu.VMEM(shape, BF16),
            pltpu.SemaphoreType.DMA(shape[:3]),
            pltpu.SemaphoreType.DMA((MINE,)),
        ],
        compiler_params=ALONE,
        cost_estimate=cost(math.prod(shape) * 6),
        name="pack_qg",
    )(place, queries, gradients)


def attend(i, slot, place, qg_mine, qg_theirs, rows_mine, rows_theirs, kv_mine, kv_theirs, far_mine, far_theirs, query_grad, sent_dq):
    tokens, width = kv_mine.shape[2:]
    half = tokens // 2
    first = query_grad is None

    def body(place_ref, qm, qt, rm, rt, km, kt_, fm, ft, *rest):
        own, far, dq_out, dq_sent = rest[-17:-13]
        qg, rows_buf, keys, buf, low, sums, far_buf, in_sem, q_sem, sem, low_sem, own_sem, far_sem = rest[-13:]
        pos = place_ref[0]
        core = lax.rem(pos, 2)
        gate = jnp.where(pos >= 2, 0.0, 1e30).astype(F32)
        head = core * MINE + i
        sides = ((core, 0), (1 - core, 1))
        copy = pltpu.make_async_copy
        loads = [copy((rm, rt)[x], rows_buf.at[n], in_sem.at[x]) for n, x in sides]
        loads += [copy((km, kt_)[x].at[i], keys.at[0, n], in_sem.at[2 + x]) for n, x in sides]
        loads += [copy((fm, ft)[x].at[slot], keys.at[1, n], in_sem.at[4 + x]) for n, x in sides]

        def q_loads(j):
            return [
                copy(qm.at[i, j], qg.at[j, core], q_sem.at[j, 0]),
                copy(qt.at[i, j], qg.at[j, 1 - core], q_sem.at[j, 1]),
            ]

        def dq_copies(j):
            return [
                copy(buf.at[core, j], dq_out.at[:, 2 * head + j, 0, :], sem.at[j]),
                copy(low.at[1 - core, j], dq_sent.at[i, j], low_sem.at[j]),
            ]

        for c in loads + q_loads(0) + q_loads(1):
            c.start()
        for c in loads:
            c.wait()
        rows = lax.broadcasted_iota(jnp.int32, (half, half), 0)
        cols = lax.broadcasted_iota(jnp.int32, (half, half), 1)
        later = rows > cols
        cut = [(a // 2, slice((a % 2) * half, (a % 2 + 1) * half)) for a in range(4)]
        tiles = [(e, a) for e in range(2) for a in range(4)]

        def one_head(j, _):
            kb = {(e, a): keys[e, cut[a][0], 0, cut[a][1], :] for e, a in tiles}
            vb = {(e, a): keys[e, cut[a][0], 1, cut[a][1], :] for e, a in tiles}
            kt = {x: kb[x].T for x in tiles}
            dk, dv = {x: [] for x in tiles}, {x: [] for x in tiles}
            for c in q_loads(j):
                c.wait()
            row = pl.ds(2 * head + j, 1)
            for b, (n, sl) in enumerate(cut):
                q, g = qg[j, n, 0, sl, :], qg[j, n, 1, sl, :]
                l = rows_buf[n, 0, row, sl] * LOG2E
                d = rows_buf[n, 1, row, sl]
                dqt = []
                for e, a in [(0, a) for a in range(b + 1)] + [(1, a) for a in range(b, 4)]:
                    p = jnp.exp2(dot(kb[e, a], q, NT) * (SCALE * LOG2E) - (l + gate if e else l))
                    if a == b:
                        p = jnp.where(later, p, 0.0) if e else jnp.where(later, 0.0, p)
                    ds = (p * (dot(vb[e, a], g, NT) - d)).astype(BF16)
                    dv[e, a].append((p.astype(BF16), g))
                    dk[e, a].append((ds, q))
                    dqt.append((kt[e, a], ds))
                x = (sum(dot(x, y, NN) for x, y in dqt) * SCALE).T
                buf[n, j, sl, :] = x
                low[n, j, sl, :] = x.astype(BF16)
            for c in dq_copies(j):
                c.start()
            for e, a in tiles:
                where = slice(a * half, (a + 1) * half)
                for t in range(2):
                    x = sum(dot(x, y, NN) for x, y in (dv if t else dk)[e, a])
                    x = (x if t else x * SCALE) + jnp.where(j == 0, 0.0, sums[e, t, where, :])
                    sums[e, t, where, :] = x
                    if e:
                        far_buf[t, where, :] = x.astype(BF16)
            return 0

        lax.fori_loop(0, 2, one_head, 0)
        out_copies = [copy(sums.at[0], own, own_sem), copy(far_buf, far, far_sem)]
        for c in out_copies:
            c.start()
        for c in dq_copies(0) + dq_copies(1) + out_copies:
            c.wait()

    operands = [place, qg_mine, qg_theirs, rows_mine, rows_theirs, kv_mine, kv_theirs, far_mine, far_theirs]
    in_specs = [SCALAR] + [HBM] * 8
    if not first:
        operands += [query_grad, sent_dq]
        in_specs += [HBM, HBM]
    return pl.pallas_call(
        body,
        in_specs=in_specs,
        out_specs=[HBM] * 4,
        out_shape=[
            like((2, 2 * tokens, width), F32),
            like((2, 2 * tokens, width), BF16),
            like((tokens, 4 * MINE, 1, width), F32),
            like((MINE, 2, tokens, width), BF16),
        ],
        scratch_shapes=[
            pltpu.VMEM((2, 2, 2, tokens, width), BF16),
            pltpu.VMEM((2, *rows_mine.shape), F32),
            pltpu.VMEM((2, 2, 2, tokens, width), BF16),
            pltpu.VMEM((2, 2, tokens, width), F32),
            pltpu.VMEM((2, 2, tokens, width), BF16),
            pltpu.VMEM((2, 2, 2 * tokens, width), F32),
            pltpu.VMEM((2, 2 * tokens, width), BF16),
            pltpu.SemaphoreType.DMA((6,)),
            pltpu.SemaphoreType.DMA((2, 2)),
            pltpu.SemaphoreType.DMA((2,)),
            pltpu.SemaphoreType.DMA((2,)),
            pltpu.SemaphoreType.DMA,
            pltpu.SemaphoreType.DMA,
        ],
        input_output_aliases={} if first else {9: 2, 10: 3},
        compiler_params=PARAMS,
        cost_estimate=cost(tokens * width * 40, 2 * 20 * 5 * 2 * half**2 * width, 2 * 20 * half**2),
        name="attend",
    )(*operands)


def finish(heads, place, owns, backs, key_grad, value_grad):
    tokens, width = owns[0].shape[1] // 2, owns[0].shape[2]
    n = len(heads)
    first = key_grad is None

    def body(place_ref, *rest):
        own_refs, back_refs, (dk, dv, send) = rest[:n], rest[n : 2 * n], rest[-10:-7]
        own_buf, back_buf, out_buf, low, in_sem, out_sem, low_sem = rest[-7:]
        core = lax.rem(place_ref[0], 2)
        order = [(x, side, t) for x in range(n) for side in range(2) for t in range(2)]

        def loads(x, side, t):
            where = pl.ds(pl.multiple_of((core if side else 1 - core) * tokens, tokens), tokens)
            return [
                pltpu.make_async_copy(own_refs[x].at[t, where, :], own_buf.at[x, side, t], in_sem.at[0, x, side, t]),
                pltpu.make_async_copy(back_refs[x].at[t, where, :], back_buf.at[x, side, t], in_sem.at[1, x, side, t]),
            ]

        for o in order:
            for c in loads(*o):
                c.start()
        waits = []
        for x, side, t in order:
            for c in loads(x, side, t):
                c.wait()
            total = own_buf[x, side, t] + back_buf[x, side, t].astype(F32)
            if side:
                out_buf[x, t] = total
                target = (dk, dv)[t].at[:, core * MINE + heads[x], 0, :]
                waits.append(pltpu.make_async_copy(out_buf.at[x, t], target, out_sem.at[x, t]))
            else:
                low[x, t] = total.astype(BF16)
                waits.append(pltpu.make_async_copy(low.at[x, t], send.at[x, t], low_sem.at[x, t]))
            waits[-1].start()
        for w in waits:
            w.wait()

    operands = [place, *owns, *backs]
    in_specs = [SCALAR] + [HBM] * (2 * n)
    if not first:
        operands += [key_grad, value_grad]
        in_specs += [HBM, HBM]
    return pl.pallas_call(
        body,
        in_specs=in_specs,
        out_specs=[HBM] * 3,
        out_shape=[like((tokens, 2 * MINE, 1, width), F32)] * 2 + [like((n, 2, tokens, width), BF16)],
        scratch_shapes=[
            pltpu.VMEM((n, 2, 2, tokens, width), F32),
            pltpu.VMEM((n, 2, 2, tokens, width), BF16),
            pltpu.VMEM((n, 2, tokens, width), F32),
            pltpu.VMEM((n, 2, tokens, width), BF16),
            pltpu.SemaphoreType.DMA((2, n, 2, 2)),
            pltpu.SemaphoreType.DMA((n, 2)),
            pltpu.SemaphoreType.DMA((n, 2)),
        ],
        input_output_aliases={} if first else {1 + 2 * n: 0, 2 + 2 * n: 1},
        compiler_params=PARAMS,
        cost_estimate=cost(n * tokens * width * 36),
        name="finish",
    )(*operands)


def write(heads, per_head, place, received, outs):
    n, _, tokens, width = received.shape

    def body(place_ref, src, *rest):
        targets, (low, wide, in_sem, out_sem) = rest[len(outs) : 2 * len(outs)], rest[2 * len(outs) :]
        other = 1 - lax.rem(place_ref[0], 2)
        loads = [pltpu.make_async_copy(src.at[x], low.at[x], in_sem.at[x]) for x in range(n)]
        for c in loads:
            c.start()
        waits = []
        for x in range(n):
            loads[x].wait()
            for t in range(2):
                wide[x, t] = low[x, t].astype(F32)
                head = other * MINE + heads[x]
                target = targets[0].at[:, 2 * head + t, 0, :] if per_head == 2 else targets[t].at[:, head, 0, :]
                waits.append(pltpu.make_async_copy(wide.at[x, t], target, out_sem.at[x, t]))
                waits[-1].start()
        for w in waits:
            w.wait()

    return pl.pallas_call(
        body,
        in_specs=[SCALAR, HBM] + [HBM] * len(outs),
        out_specs=[HBM] * len(outs),
        out_shape=[like(o.shape, F32) for o in outs],
        scratch_shapes=[
            pltpu.VMEM((n, 2, tokens, width), BF16),
            pltpu.VMEM((n, 2, tokens, width), F32),
            pltpu.SemaphoreType.DMA((n,)),
            pltpu.SemaphoreType.DMA((n, 2)),
        ],
        input_output_aliases={2 + i: i for i in range(len(outs))},
        compiler_params=PARAMS,
        cost_estimate=cost(n * tokens * width * 12),
        name="write",
    )(place, received, *outs)


def terms(query_tensor, key_tensor, value_tensor, output_gradient, logsumexp, row_inner_products):
    tokens, qheads, width = query_tensor.shape
    kheads = key_tensor.shape[1]
    place = lax.axis_index("seq").astype(jnp.int32).reshape(1)
    queries, gradients = (x.reshape(tokens, qheads, 1, width) for x in (query_tensor, output_gradient))
    keys, values = (x.reshape(tokens, kheads, 1, width) for x in (key_tensor, value_tensor))
    kv_mine, *parts, rows_mine = pack_kv(place, keys, values, logsumexp, row_inner_products)
    kv_give = parts.pop()
    groups = len(GROUPS)
    far = []
    for c in range(groups):
        far.append((rotated(parts[c], 2), crossed(parts[groups + c], 2)))
    kv_theirs = partner(kv_give)
    rows_theirs = partner(rows_mine)
    qg_give = pack_qg(True, place, queries, gradients)
    qg_theirs = partner(qg_give)
    qg_mine = pack_qg(False, place, queries, gradients)
    shared = (place, qg_mine, qg_theirs, rows_mine, rows_theirs, kv_mine, kv_theirs)
    query_grad = sent_dq = None
    own, back = [], []
    for c, size in enumerate(GROUPS):
        for slot in range(size):
            h = len(own)
            mine, theirs, query_grad, sent_dq = attend(h, slot, *shared, *far[c], query_grad, sent_dq)
            own.append(mine)
            back.append(rotated(theirs, -2))
    got_dq = partner(sent_dq)
    (query_grad,) = write(range(MINE), 2, place, got_dq, [query_grad])
    early = range(MINE - 1)
    key_grad, value_grad, send = finish(early, place, own[:-1], back[:-1], None, None)
    got = partner(send)
    key_grad, value_grad = write(early, 1, place, got, [key_grad, value_grad])
    last = [MINE - 1]
    key_grad, value_grad, send = finish(last, place, own[-1:], back[-1:], key_grad, value_grad)
    got = partner(send)
    key_grad, value_grad = write(last, 1, place, got, [key_grad, value_grad])
    return (
        query_grad.reshape(tokens, qheads, width),
        key_grad.reshape(tokens, kheads, width),
        value_grad.reshape(tokens, kheads, width),
    )


def solution(mesh):
    return jax.shard_map(
        terms,
        mesh=mesh,
        in_specs=(
            P("seq", "head", None),
            P("seq", "head", None),
            P("seq", "head", None),
            P("seq", "head", None),
            P("head", "seq"),
            P("head", "seq"),
        ),
        out_specs=(P("seq", "head", None), P("seq", "head", None), P("seq", "head", None)),
        check_vma=False,
    )
```

profile of v0, /device:TPU:6, one launch (start us, length us, event | category | flops | bytes accessed | tf_op | source)
XLA Modules:
  0.0 137.3 jit_solution(37045634472805366)
XLA Ops:
  0.6 3.7 %pack_qg.3 = bf16[4,2,2,512,128]{4,3,2,1,0:T(8,128)(2,1)} custom-call(s32[1]{0:T(128)} %bitcast.place_ref, f32[512,16,1,128]{3,2,1,0:T(1,128)} %bitcast.10, f32[512,16,1,128]{3,2,1,0:T(1,128)} %bitcast.12), custom_call_target="tpu_custom_call" | custom-call | bytes 6291456 | tf_op jit(solution)/shard_map/pack_qg/pallas_call | solution.py:144
  4.4 0.1 collective-permute-start
  4.5 4.4 %pack_kv.1 = (bf16[4,2,512,128]{3,2,1,0:T(8,128)(2,1)}, bf16[1,2,512,128]{3,2,1,0:T(8,128)(2,1)}, bf16[1,2,512,128]{3,2,1,0:T(8,128)(2,1)}, bf16[1,2,512,128]{3,...) custom-call(s32[1]{0:T(128)} %bitcast.place_ref, ...), custom_call_target="tpu_custom_call" | custom-call | bytes 6291456 | tf_op jit(solution)/shard_map/pack_kv/pallas_call | solution.py:92
  8.8 0.6 collective-permute-start.2
  9.4 1.3 collective-permute-start.10
  10.7 1.6 %collective-permute-start.9 = (bf16[1,2,512,128]{3,2,1,0:T(8,128)(2,1)}, bf16[1,2,512,128]{3,2,1,0:T(8,128)(2,1)}, u32[]{:S(2)}, u32[]{:S(2)}) collective-permute-start(bf16[1,2,512,128]{3,2,1,0:T(8,128)(2,1)} %get-tuple-element.49), channel_id=1, source_target_pairs={{0,4},{2,6},{4,8},{6,10},{8,12},{10,14},{12,16},{14,18},{16,20},{1... | collective-permute-start | bytes 786440 | tf_op jit(solution)/shard_map/ppermute | solution.py:33
  12.2 0.1 collective-permute-start.1
  12.4 3.8 %pack_qg.2.qm = bf16[4,2,2,512,128]{4,3,2,1,0:T(8,128)(2,1)} custom-call(s32[1]{0:T(128)} %bitcast.place_ref, f32[512,16,1,128]{3,2,1,0:T(1,128)} %bitcast.11, f32[512,16,1,128]{3,2,1,0:T(1,128)} %bitcast.13), custom_call_target="tpu_custom_call" | custom-call | bytes 6291456 | tf_op jit(solution)/shard_map/pack_qg/pallas_call | solution.py:144
  16.2 1.4 collective-permute-start.7
  17.5 4.8 %collective-permute-done.10.ft = bf16[1,2,512,128]{3,2,1,0:T(8,128)(2,1)S(1)} collective-permute-done((bf16[1,2,512,128]{3,2,1,0:T(8,128)(2,1)}, bf16[1,2,512,128]{3,2,1,0:T(8,128)(2,1)S(1)}, u32[]{:S(2)}, u32[]{:S(2)}) %collective-permute-start.10) | collective-permute-done | bytes 262176 | tf_op jit(solution)/shard_map/ppermute | solution.py:38
  22.3 6.9 %collective-permute-done.9.fm = bf16[1,2,512,128]{3,2,1,0:T(8,128)(2,1)} collective-permute-done((bf16[1,2,512,128]{3,2,1,0:T(8,128)(2,1)}, bf16[1,2,512,128]{3,2,1,0:T(8,128)(2,1)}, u32[]{:S(2)}, u32[]{:S(2)}) %collective-permute-start.9) | collective-permute-done | bytes 262176 | tf_op jit(solution)/shard_map/ppermute | solution.py:33
  29.3 1.6 %copy-done = bf16[4,2,2,512,128]{4,3,2,1,0:T(8,128)(2,1)S(1)} copy-done((bf16[4,2,2,512,128]{4,3,2,1,0:T(8,128)(2,1)S(1)}, bf16[4,2,2,512,128]{4,3,2,1,0:T(8,128)(2,1)}, u32[]{:S(2)}) %copy-start) | copy-done | bytes 2097176
  30.9 9.4 %attend.4 = (f32[2,1024,128]{2,1,0:T(8,128)S(1)}, bf16[2,1024,128]{2,1,0:T(8,128)(2,1)S(1)}, f32[512,16,1,128]{3,2,1,0:T(1,128)}, bf16[4,2,512,128]{3,2,1,0:T(8,128)(2,1)S(1)}) custom-call(s32[1]{0:T(128)} %bitcast.place_ref, bf16[4,2,2,512,128]{4,3,2,1,0:T(8,128)(2,1)S(1)} %copy-done, bf16[4,2,2,512,128]{4,3,2,1,0:T(8,128)(2,1)} %collective-permute-done.qt, ...), custom_call_target="tpu_custom_call" | custom-call | flops 3355443200 | bytes 2621440 | tf_op jit(solution)/shard_map/attend/pallas_call | solution.py:249
  40.4 9.4 %attend.5 = (f32[2,1024,128]{2,1,0:T(8,128)S(1)}, bf16[2,1024,128]{2,1,0:T(8,128)(2,1)S(1)}, f32[512,16,1,128]{3,2,1,0:T(1,128)}, bf16[4,2,512,128]{3,2,1,0:T(8,128)(2,1)S(1)}) custom-call(s32[1]{0:T(128)} %bitcast.place_ref, bf16[4,2,2,512,128]{4,3,2,1,0:T(8,128)(2,1)S(1)} %copy-done, ...), custom_call_target="tpu_custom_call", output_to_operand_aliasing={{2}: (9, {}), {3}: (10, {})} | custom-call | flops 3355443200 | bytes 2621440 | tf_op jit(solution)/shard_map/attend/pallas_call | solution.py:249
  49.8 0.6 collective-permute-done.6.ft
  50.4 9.4 %attend.6 = (f32[2,1024,128]{2,1,0:T(8,128)S(1)}, bf16[2,1024,128]{2,1,0:T(8,128)(2,1)S(1)}, f32[512,16,1,128]{3,2,1,0:T(1,128)}, bf16[4,2,512,128]{3,2,1,0:T(8,128)(2,1)S(1)}) custom-call(s32[1]{0:T(128)} %bitcast.place_ref, bf16[4,2,2,512,128]{4,3,2,1,0:T(8,128)(2,1)S(1)} %copy-done, ...), custom_call_target="tpu_custom_call", output_to_operand_aliasing={{2}: (9, {}), {3}: (10, {})} | custom-call | flops 3355443200 | bytes 2621440 | tf_op jit(solution)/shard_map/attend/pallas_call | solution.py:249
  59.8 6.0 %collective-permute-start.15 = (bf16[2,1024,128]{2,1,0:T(8,128)(2,1)S(1)}, bf16[2,1024,128]{2,1,0:T(8,128)(2,1)S(1)}, u32[]{:S(2)}, u32[]{:S(2)}) collective-permute-start(bf16[2,1024,128]{2,1,0:T(8,128)(2,1)S(1)} %get-tuple-element.66), channel_id=1, source_target_pairs={{0,124},{2,126},{4,0},{6,2},{8,4},{10,6},{12,8},{14,10},{16,12},{1... | collective-permute-start | bytes 1572872 | tf_op jit(solution)/shard_map/ppermute | solution.py:33
  65.7 0.2 collective-permute-start.14
  66.1 1.9 %collective-permute-start.3 = (bf16[1,2,512,128]{3,2,1,0:T(8,128)(2,1)S(1)}, bf16[1,2,512,128]{3,2,1,0:T(8,128)(2,1)S(1)}, u32[]{:S(2)}, u32[]{:S(2)}) collective-permute-start(bf16[1,2,512,128]{3,2,1,0:T(8,128)(2,1)S(1)} %copy-done.5), channel_id=1, source_target_pairs={{0,4},{2,6},{4,8},{6,10},{8,12},{10,14},{12,16},{14,18},{16,20},{1... | collective-permute-start | bytes 786440 | tf_op jit(solution)/shard_map/ppermute | solution.py:33
  68.0 0.7 collective-permute-start.4
  68.7 9.3 %collective-permute-done.15.rest_5_ = bf16[2,1024,128]{2,1,0:T(8,128)(2,1)S(1)} collective-permute-done((bf16[2,1024,128]{2,1,0:T(8,128)(2,1)S(1)}, bf16[2,1024,128]{2,1,0:T(8,128)(2,1)S(1)}, u32[]{:S(2)}, u32[]{:S(2)}) %collective-permute-start.15) | collective-permute-done | bytes 524320 | tf_op jit(solution)/shard_map/ppermute | solution.py:33
  78.1 11.2 %collective-permute-done.14.rest_4_ = bf16[2,1024,128]{2,1,0:T(8,128)(2,1)S(1)} collective-permute-done((bf16[2,1024,128]{2,1,0:T(8,128)(2,1)S(1)}, bf16[2,1024,128]{2,1,0:T(8,128)(2,1)S(1)}, u32[]{:S(2)}, u32[]{:S(2)}) %collective-permute-start.14) | collective-permute-done | bytes 524320 | tf_op jit(solution)/shard_map/ppermute | solution.py:33
  89.3 10.4 %collective-permute-done.13.rest_3_ = bf16[2,1024,128]{2,1,0:T(8,128)(2,1)S(1)} collective-permute-done((bf16[2,1024,128]{2,1,0:T(8,128)(2,1)S(1)}, bf16[2,1024,128]{2,1,0:T(8,128)(2,1)S(1)}, u32[]{:S(2)}, u32[]{:S(2)}) %collective-permute-start.13) | collective-permute-done | bytes 524320 | tf_op jit(solution)/shard_map/ppermute | solution.py:33
  99.7 4.7 %finish.2 = (f32[512,8,1,128]{3,2,1,0:T(1,128)}, f32[512,8,1,128]{3,2,1,0:T(1,128)}, bf16[3,2,512,128]{3,2,1,0:T(8,128)(2,1)S(1)}) custom-call(s32[1]{0:T(128)} %bitcast.place_ref, f32[2,1024,128]{2,1,0:T(8,128)S(1)} %get-tuple-element.61.rest_0_, f32[2,1024,128]{2,1,0:T(8,128)S(1)} %get-tuple-element.62.rest_1_, ...), custom_call_target="tpu_custom_call" | custom-call | bytes 7077888 | tf_op jit(solution)/shard_map/finish/pallas_call | solution.py:323
  104.5 9.4 %attend.7 = (f32[2,1024,128]{2,1,0:T(8,128)S(1)}, bf16[2,1024,128]{2,1,0:T(8,128)(2,1)S(1)}, f32[512,16,1,128]{3,2,1,0:T(1,128)}, bf16[4,2,512,128]{3,2,1,0:T(8,128)(2,1)S(1)}) custom-call(s32[1]{0:T(128)} %bitcast.place_ref, bf16[4,2,2,512,128]{4,3,2,1,0:T(8,128)(2,1)S(1)} %copy-done.1, ...), custom_call_target="tpu_custom_call", output_to_operand_aliasing={{2}: (9, {}), {3}: (10, {})} | custom-call | flops 3355443200 | bytes 2621440 | tf_op jit(solution)/shard_map/attend/pallas_call | solution.py:249
  113.9 0.6 collective-permute-start.11
  114.4 6.7 %collective-permute-start.12 = (bf16[2,1024,128]{2,1,0:T(8,128)(2,1)S(1)}, bf16[2,1024,128]{2,1,0:T(8,128)(2,1)S(1)}, u32[]{:S(2)}, u32[]{:S(2)}) collective-permute-start(bf16[2,1024,128]{2,1,0:T(8,128)(2,1)S(1)} %get-tuple-element.60), channel_id=1, source_target_pairs={{0,124},{2,126},{4,0},{6,2},{8,4},{10,6},{12,8},{14,10},{16,12},{1... | collective-permute-start | bytes 1572872 | tf_op jit(solution)/shard_map/ppermute | solution.py:33
  121.1 1.3 write.4
  122.4 10.1 %collective-permute-done.12.rest_1_ = bf16[2,1024,128]{2,1,0:T(8,128)(2,1)S(1)} collective-permute-done((bf16[2,1024,128]{2,1,0:T(8,128)(2,1)S(1)}, bf16[2,1024,128]{2,1,0:T(8,128)(2,1)S(1)}, u32[]{:S(2)}, u32[]{:S(2)}) %collective-permute-start.12) | collective-permute-done | bytes 524320 | tf_op jit(solution)/shard_map/ppermute | solution.py:33
  132.6 2.1 %finish.3 = (f32[512,8,1,128]{3,2,1,0:T(1,128)}, f32[512,8,1,128]{3,2,1,0:T(1,128)}, bf16[1,2,512,128]{3,2,1,0:T(8,128)(2,1)S(1)}) custom-call(s32[1]{0:T(128)} %bitcast.place_ref, f32[2,1024,128]{2,1,0:T(8,128)S(1)} %get-tuple-element.59.rest_0_, ...), custom_call_target="tpu_custom_call", output_to_operand_aliasing={{0}: (3, {}), {1}: (4, {})} | custom-call | bytes 2359296 | tf_op jit(solution)/shard_map/finish/pallas_call | solution.py:323
  134.7 1.5 %write.3 = f32[512,16,1,128]{3,2,1,0:T(1,128)} custom-call(s32[1]{0:T(128)} %bitcast.place_ref, bf16[4,2,512,128]{3,2,1,0:T(8,128)(2,1)S(1)} %collective-permute-done.11.src, f32[512,16,1,128]{3,2,1,0:T(1,128)} %get-tuple-element.58.rest_0_), custom_call_target="tpu_custom_call", output_to_operand_aliasing={{}: (2, {})} | custom-call | bytes 3145728 | tf_op jit(solution)/shard_map/write/pallas_call | solution.py:365
  136.2 0.9 write.5
  (28 shorter events, 0.3 us)
Async XLA Ops:
  4.4 24.9 %collective-permute-start = (bf16[4,2,2,512,128]{4,3,2,1,0:T(8,128)(2,1)}, bf16[4,2,2,512,128]{4,3,2,1,0:T(8,128)(2,1)}, u32[]{:S(2)}, u32[]{:S(2)}) collective-permute-start(bf16[4,2,2,512,128]{4,3,2,1,0:T(8,128)(2,1)} %pack_qg.3), channel_id=1, source_target_pairs={{0,2},{2,0},{4,6},{6,4},{8,10},{10,8},{12,14},{14,12},{16,18},{18,... | collective-permute-start | bytes 6291464 | tf_op jit(solution)/shard_map/ppermute | solution.py:43
  8.8 20.4 %collective-permute-start.2 = (bf16[4,2,512,128]{3,2,1,0:T(8,128)(2,1)}, bf16[4,2,512,128]{3,2,1,0:T(8,128)(2,1)}, u32[]{:S(2)}, u32[]{:S(2)}) collective-permute-start(bf16[4,2,512,128]{3,2,1,0:T(8,128)(2,1)} %get-tuple-element.42), channel_id=1, source_target_pairs={{0,2},{2,0},{4,6},{6,4},{8,10},{10,8},{12,14},{14,12},{16,18},{18,... | collective-permute-start | bytes 3145736 | tf_op jit(solution)/shard_map/ppermute | solution.py:43
  9.4 12.9 %collective-permute-start.10 = (bf16[1,2,512,128]{3,2,1,0:T(8,128)(2,1)}, bf16[1,2,512,128]{3,2,1,0:T(8,128)(2,1)S(1)}, u32[]{:S(2)}, u32[]{:S(2)}) collective-permute-start(bf16[1,2,512,128]{3,2,1,0:T(8,128)(2,1)} %get-tuple-element.50), channel_id=1, source_target_pairs={{0,6},{2,4},{4,10},{6,8},{8,14},{10,12},{12,18},{14,16},{16,22},{1... | collective-permute-start | bytes 786440 | tf_op jit(solution)/shard_map/ppermute | solution.py:38
  10.7 18.6 %collective-permute-start.9 = (bf16[1,2,512,128]{3,2,1,0:T(8,128)(2,1)}, bf16[1,2,512,128]{3,2,1,0:T(8,128)(2,1)}, u32[]{:S(2)}, u32[]{:S(2)}) collective-permute-start(bf16[1,2,512,128]{3,2,1,0:T(8,128)(2,1)} %get-tuple-element.49), channel_id=1, source_target_pairs={{0,4},{2,6},{4,8},{6,10},{8,12},{10,14},{12,16},{14,18},{16,20},{1... | collective-permute-start | bytes 786440 | tf_op jit(solution)/shard_map/ppermute | solution.py:33
  12.2 17.0 %copy-start.2 = (bf16[4,2,512,128]{3,2,1,0:T(8,128)(2,1)S(1)}, bf16[4,2,512,128]{3,2,1,0:T(8,128)(2,1)}, u32[]{:S(2)}) copy-start(bf16[4,2,512,128]{3,2,1,0:T(8,128)(2,1)} %get-tuple-element.41.km) | copy-start | bytes 3145732
  12.2 17.0 %copy-start.3 = (f32[2,16,512]{2,1,0:T(8,128)S(1)}, f32[2,16,512]{2,1,0:T(8,128)}, u32[]{:S(2)}) copy-start(f32[2,16,512]{2,1,0:T(8,128)} %get-tuple-element.40.rm) | copy-start | bytes 196612
  12.2 3.9 %collective-permute-start.1 = (f32[2,16,512]{2,1,0:T(8,128)}, f32[2,16,512]{2,1,0:T(8,128)S(1)}, u32[]{:S(2)}, u32[]{:S(2)}) collective-permute-start(f32[2,16,512]{2,1,0:T(8,128)} %get-tuple-element.40.rm), channel_id=1, source_target_pairs={{0,2},{2,0},{4,6},{6,4},{8,10},{10,8},{12,14},{14,12},{16,18},{18,... | collective-permute-start | bytes 196616 | tf_op jit(solution)/shard_map/ppermute | solution.py:43
  16.2 24.1 %collective-permute-start.7 = (bf16[1,2,512,128]{3,2,1,0:T(8,128)(2,1)}, bf16[1,2,512,128]{3,2,1,0:T(8,128)(2,1)S(1)}, u32[]{:S(2)}, u32[]{:S(2)}) collective-permute-start(bf16[1,2,512,128]{3,2,1,0:T(8,128)(2,1)} %get-tuple-element.47), channel_id=1, source_target_pairs={{0,4},{2,6},{4,8},{6,10},{8,12},{10,14},{12,16},{14,18},{16,20},{1... | collective-permute-start | bytes 786440 | tf_op jit(solution)/shard_map/ppermute | solution.py:33
  22.3 18.0 %collective-permute-start.8 = (bf16[1,2,512,128]{3,2,1,0:T(8,128)(2,1)}, bf16[1,2,512,128]{3,2,1,0:T(8,128)(2,1)S(1)}, u32[]{:S(2)}, u32[]{:S(2)}) collective-permute-start(bf16[1,2,512,128]{3,2,1,0:T(8,128)(2,1)} %get-tuple-element.48), channel_id=1, source_target_pairs={{0,6},{2,4},{4,10},{6,8},{8,14},{10,12},{12,18},{14,16},{16,22},{1... | collective-permute-start | bytes 786440 | tf_op jit(solution)/shard_map/ppermute | solution.py:38
  29.2 20.5 %collective-permute-start.5 = (bf16[1,2,512,128]{3,2,1,0:T(8,128)(2,1)}, bf16[1,2,512,128]{3,2,1,0:T(8,128)(2,1)S(1)}, u32[]{:S(2)}, u32[]{:S(2)}) collective-permute-start(bf16[1,2,512,128]{3,2,1,0:T(8,128)(2,1)} %get-tuple-element.45), channel_id=1, source_target_pairs={{0,4},{2,6},{4,8},{6,10},{8,12},{10,14},{12,16},{14,18},{16,20},{1... | collective-permute-start | bytes 786440 | tf_op jit(solution)/shard_map/ppermute | solution.py:33
  29.2 21.1 %collective-permute-start.6 = (bf16[1,2,512,128]{3,2,1,0:T(8,128)(2,1)}, bf16[1,2,512,128]{3,2,1,0:T(8,128)(2,1)S(1)}, u32[]{:S(2)}, u32[]{:S(2)}) collective-permute-start(bf16[1,2,512,128]{3,2,1,0:T(8,128)(2,1)} %get-tuple-element.46), channel_id=1, source_target_pairs={{0,6},{2,4},{4,10},{6,8},{8,14},{10,12},{12,18},{14,16},{16,22},{1... | collective-permute-start | bytes 786440 | tf_op jit(solution)/shard_map/ppermute | solution.py:38
  29.3 1.6 %copy-start = (bf16[4,2,2,512,128]{4,3,2,1,0:T(8,128)(2,1)S(1)}, bf16[4,2,2,512,128]{4,3,2,1,0:T(8,128)(2,1)}, u32[]{:S(2)}) copy-start(bf16[4,2,2,512,128]{4,3,2,1,0:T(8,128)(2,1)} %pack_qg.2.qm) | copy-start | bytes 6291460
  50.4 15.7 %copy-start.5 = (bf16[1,2,512,128]{3,2,1,0:T(8,128)(2,1)S(1)}, bf16[1,2,512,128]{3,2,1,0:T(8,128)(2,1)}, u32[]{:S(2)}) copy-start(bf16[1,2,512,128]{3,2,1,0:T(8,128)(2,1)} %get-tuple-element.43) | copy-start | bytes 786436
  50.4 17.6 %copy-start.4 = (bf16[1,2,512,128]{3,2,1,0:T(8,128)(2,1)S(1)}, bf16[1,2,512,128]{3,2,1,0:T(8,128)(2,1)}, u32[]{:S(2)}) copy-start(bf16[1,2,512,128]{3,2,1,0:T(8,128)(2,1)} %get-tuple-element.44) | copy-start | bytes 786436
  59.8 18.3 %collective-permute-start.15 = (bf16[2,1024,128]{2,1,0:T(8,128)(2,1)S(1)}, bf16[2,1024,128]{2,1,0:T(8,128)(2,1)S(1)}, u32[]{:S(2)}, u32[]{:S(2)}) collective-permute-start(bf16[2,1024,128]{2,1,0:T(8,128)(2,1)S(1)} %get-tuple-element.66), channel_id=1, source_target_pairs={{0,124},{2,126},{4,0},{6,2},{8,4},{10,6},{12,8},{14,10},{16,12},{1... | collective-permute-start | bytes 1572872 | tf_op jit(solution)/shard_map/ppermute | solution.py:33
  65.7 23.6 %collective-permute-start.14 = (bf16[2,1024,128]{2,1,0:T(8,128)(2,1)S(1)}, bf16[2,1024,128]{2,1,0:T(8,128)(2,1)S(1)}, u32[]{:S(2)}, u32[]{:S(2)}) collective-permute-start(bf16[2,1024,128]{2,1,0:T(8,128)(2,1)S(1)} %get-tuple-element.65), channel_id=1, source_target_pairs={{0,124},{2,126},{4,0},{6,2},{8,4},{10,6},{12,8},{14,10},{16,12},{1... | collective-permute-start | bytes 1572872 | tf_op jit(solution)/shard_map/ppermute | solution.py:33
  66.0 33.7 %collective-permute-start.13 = (bf16[2,1024,128]{2,1,0:T(8,128)(2,1)S(1)}, bf16[2,1024,128]{2,1,0:T(8,128)(2,1)S(1)}, u32[]{:S(2)}, u32[]{:S(2)}) collective-permute-start(bf16[2,1024,128]{2,1,0:T(8,128)(2,1)S(1)} %get-tuple-element.64), channel_id=1, source_target_pairs={{0,124},{2,126},{4,0},{6,2},{8,4},{10,6},{12,8},{14,10},{16,12},{1... | collective-permute-start | bytes 1572872 | tf_op jit(solution)/shard_map/ppermute | solution.py:33
  66.1 38.4 %collective-permute-start.3 = (bf16[1,2,512,128]{3,2,1,0:T(8,128)(2,1)S(1)}, bf16[1,2,512,128]{3,2,1,0:T(8,128)(2,1)S(1)}, u32[]{:S(2)}, u32[]{:S(2)}) collective-permute-start(bf16[1,2,512,128]{3,2,1,0:T(8,128)(2,1)S(1)} %copy-done.5), channel_id=1, source_target_pairs={{0,4},{2,6},{4,8},{6,10},{8,12},{10,14},{12,16},{14,18},{16,20},{1... | collective-permute-start | bytes 786440 | tf_op jit(solution)/shard_map/ppermute | solution.py:33
  68.0 36.4 %collective-permute-start.4 = (bf16[1,2,512,128]{3,2,1,0:T(8,128)(2,1)S(1)}, bf16[1,2,512,128]{3,2,1,0:T(8,128)(2,1)S(1)}, u32[]{:S(2)}, u32[]{:S(2)}) collective-permute-start(bf16[1,2,512,128]{3,2,1,0:T(8,128)(2,1)S(1)} %copy-done.4), channel_id=1, source_target_pairs={{0,6},{2,4},{4,10},{6,8},{8,14},{10,12},{12,18},{14,16},{16,22},{1... | collective-permute-start | bytes 786440 | tf_op jit(solution)/shard_map/ppermute | solution.py:38
  99.7 4.8 %copy-start.1 = (bf16[4,2,2,512,128]{4,3,2,1,0:T(8,128)(2,1)S(1)}, bf16[4,2,2,512,128]{4,3,2,1,0:T(8,128)(2,1)}, u32[]{:S(2)}) copy-start(bf16[4,2,2,512,128]{4,3,2,1,0:T(8,128)(2,1)} %pack_qg.2.qm) | copy-start | bytes 6291460
  104.3 16.8 %collective-permute-start.16 = (bf16[3,2,512,128]{3,2,1,0:T(8,128)(2,1)S(1)}, bf16[3,2,512,128]{3,2,1,0:T(8,128)(2,1)S(1)}, u32[]{:S(2)}, u32[]{:S(2)}) collective-permute-start(bf16[3,2,512,128]{3,2,1,0:T(8,128)(2,1)S(1)} %get-tuple-element.67), channel_id=1, source_target_pairs={{0,2},{2,0},{4,6},{6,4},{8,10},{10,8},{12,14},{14,12},{16,18},{18,... | collective-permute-start | bytes 2359304 | tf_op jit(solution)/shard_map/ppermute | solution.py:43
  113.9 20.8 %collective-permute-start.11 = (bf16[4,2,512,128]{3,2,1,0:T(8,128)(2,1)S(1)}, bf16[4,2,512,128]{3,2,1,0:T(8,128)(2,1)S(1)}, u32[]{:S(2)}, u32[]{:S(2)}) collective-permute-start(bf16[4,2,512,128]{3,2,1,0:T(8,128)(2,1)S(1)} %get-tuple-element.57), channel_id=1, source_target_pairs={{0,2},{2,0},{4,6},{6,4},{8,10},{10,8},{12,14},{14,12},{16,18},{18,... | collective-permute-start | bytes 3145736 | tf_op jit(solution)/shard_map/ppermute | solution.py:43
  114.4 18.1 %collective-permute-start.12 = (bf16[2,1024,128]{2,1,0:T(8,128)(2,1)S(1)}, bf16[2,1024,128]{2,1,0:T(8,128)(2,1)S(1)}, u32[]{:S(2)}, u32[]{:S(2)}) collective-permute-start(bf16[2,1024,128]{2,1,0:T(8,128)(2,1)S(1)} %get-tuple-element.60), channel_id=1, source_target_pairs={{0,124},{2,126},{4,0},{6,2},{8,4},{10,6},{12,8},{14,10},{16,12},{1... | collective-permute-start | bytes 1572872 | tf_op jit(solution)/shard_map/ppermute | solution.py:33
  134.6 1.6 %collective-permute-start.17 = (bf16[1,2,512,128]{3,2,1,0:T(8,128)(2,1)S(1)}, bf16[1,2,512,128]{3,2,1,0:T(8,128)(2,1)S(1)}, u32[]{:S(2)}, u32[]{:S(2)}) collective-permute-start(bf16[1,2,512,128]{3,2,1,0:T(8,128)(2,1)S(1)} %get-tuple-element.72), channel_id=1, source_target_pairs={{0,2},{2,0},{4,6},{6,4},{8,10},{10,8},{12,14},{14,12},{16,18},{18,... | collective-permute-start | bytes 786440 | tf_op jit(solution)/shard_map/ppermute | solution.py:43
where the time goes:
time: 140 us; the launch traced here: 137 us
  Pallas kernels  59.9 us (43%)
  waiting for transfers between devices  53.4 us (38%)
  starting transfers between devices  21.4 us (15%)
  local copies, waits for them, and re-layouts  1.6 us (1%)
    ppermute x8, waiting for transfers between devices, rotated(): return lax.ppermute(x, 'seq', [(i, (i + by) % count) for i in range(count)])  48 us
    pallas_call x4, Pallas kernels, attend(): pl.pallas_call(body, in_specs=in_specs, out_specs=[HBM] * 4, out_shape=[l...  37.7 us
    ppermute x8, starting transfers between devices, rotated(): return lax.ppermute(x, 'seq', [(i, (i + by) % count) for i in range(count)])  17.8 us
    pallas_call x2, Pallas kernels, pack_qg(): pl.pallas_call(body, in_specs=[SCALAR, GIVEN, GIVEN], out_specs=HBM, out_...  7.51 us
    pallas_call x2, Pallas kernels, finish(): pl.pallas_call(body, in_specs=in_specs, out_specs=[HBM] * 3, out_shape=[l...  6.71 us
    ppermute x4, waiting for transfers between devices, crossed(): lax.ppermute(x, 'seq', [(i, (i + by) % count ^ 1) for i in range(count)])  5.37 us
    pallas_call x1, Pallas kernels, pack_kv(): pl.pallas_call(body, in_specs=[SCALAR] + [GIVEN] * 4, out_specs=[HBM] * (...  4.36 us
    pallas_call x3, Pallas kernels, write(): pl.pallas_call(body, in_specs=[SCALAR, HBM] + [HBM] * len(outs), out_spec...  3.66 us
  transfers between devices with their start and end apart: 18, of which 7 were waited for; matrix products, arithmetic and copies ran while one was open for 0% of the time, Pallas kernels for 33%

commit v1 on v0

--- a/solution.py
+++ b/solution.py
@@ -158,14 +158,14 @@
     )(place, queries, gradients)
 
 
-def attend(i, slot, place, qg_mine, qg_theirs, rows_mine, rows_theirs, kv_mine, kv_theirs, far_mine, far_theirs, query_grad, sent_dq):
+def attend(i, slot, place, qg_mine, qg_theirs, rows_mine, rows_theirs, kv_mine, kv_theirs, far_mine, far_theirs, query_grad, sent_dq, split):
     tokens, width = kv_mine.shape[2:]
     half = tokens // 2
     first = query_grad is None
 
     def body(place_ref, qm, qt, rm, rt, km, kt_, fm, ft, *rest):
-        own, far, dq_out, dq_sent = rest[-17:-13]
-        qg, rows_buf, keys, buf, low, sums, far_buf, in_sem, q_sem, sem, low_sem, own_sem, far_sem = rest[-13:]
+        own, *others, dq_out, dq_sent = rest[-15 - (6 if split else 4) : -15]
+        qg, rows_buf, keys, buf, low, sums, far_buf, own_low, in_sem, q_sem, sem, low_sem, own_sem, far_sem, give_sem = rest[-15:]
         pos = place_ref[0]
         core = lax.rem(pos, 2)
         gate = jnp.where(pos >= 2, 0.0, 1e30).astype(F32)
@@ -232,10 +232,19 @@
                     sums[e, t, where, :] = x
                     if e:
                         far_buf[t, where, :] = x.astype(BF16)
+                    elif split:
+                        own_low[t, where, :] = x.astype(BF16)
             return 0
 
         lax.fori_loop(0, 2, one_head, 0)
-        out_copies = [copy(sums.at[0], own, own_sem), copy(far_buf, far, far_sem)]
+        out_copies = [copy(sums.at[0], own, own_sem)]
+        if split:
+            keep, give = (pl.ds(pl.multiple_of(x * tokens, tokens), tokens) for x in (core, 1 - core))
+            out_copies.append(copy(far_buf.at[:, keep, :], others[0], far_sem))
+            out_copies.append(copy(far_buf.at[:, give, :], others[1], give_sem.at[0]))
+            out_copies.append(copy(own_low.at[:, give, :], others[2], give_sem.at[1]))
+        else:
+            out_copies.append(copy(far_buf, others[0], far_sem))
         for c in out_copies:
             c.start()
         for c in dq_copies(0) + dq_copies(1) + out_copies:
@@ -249,10 +258,10 @@
     return pl.pallas_call(
         body,
         in_specs=in_specs,
-        out_specs=[HBM] * 4,
+        out_specs=[HBM] * (6 if split else 4),
         out_shape=[
             like((2, 2 * tokens, width), F32),
-            like((2, 2 * tokens, width), BF16),
+            *([like((2, tokens, width), BF16)] * 3 if split else [like((2, 2 * tokens, width), BF16)]),
             like((tokens, 4 * MINE, 1, width), F32),
             like((MINE, 2, tokens, width), BF16),
         ],
@@ -264,14 +273,16 @@
             pltpu.VMEM((2, 2, tokens, width), BF16),
             pltpu.VMEM((2, 2, 2 * tokens, width), F32),
             pltpu.VMEM((2, 2 * tokens, width), BF16),
+            pltpu.VMEM((2, 2 * tokens, width), BF16),
             pltpu.SemaphoreType.DMA((6,)),
             pltpu.SemaphoreType.DMA((2, 2)),
             pltpu.SemaphoreType.DMA((2,)),
             pltpu.SemaphoreType.DMA((2,)),
             pltpu.SemaphoreType.DMA,
             pltpu.SemaphoreType.DMA,
-        ],
-        input_output_aliases={} if first else {9: 2, 10: 3},
+            pltpu.SemaphoreType.DMA((2,)),
+        ],
+        input_output_aliases={} if first else {9: 4, 10: 5} if split else {9: 2, 10: 3},
         compiler_params=PARAMS,
         cost_estimate=cost(tokens * width * 40, 2 * 20 * 5 * 2 * half**2 * width, 2 * 20 * half**2),
         name="attend",
@@ -378,6 +389,64 @@
         cost_estimate=cost(n * tokens * width * 12),
         name="write",
     )(place, received, *outs)
+
+
+def finish_last(head, place, own, got_own, back_keep, back_cross, key_grad, value_grad):
+    tokens, width = back_keep.shape[1:]
+
+    def body(place_ref, own_ref, got_ref, keep_ref, cross_ref, *rest):
+        (dk, dv), (wide, low, out_buf, wide_sem, low_sem, out_sem) = rest[2:4], rest[4:]
+        core = lax.rem(place_ref[0], 2)
+        copy = pltpu.make_async_copy
+        mine = pl.ds(pl.multiple_of(core * tokens, tokens), tokens)
+        order = [(side, t) for t in range(2) for side in range(2)]
+
+        def loads(side, t):
+            if side:
+                return [
+                    copy(got_ref.at[t], low.at[1, t], low_sem.at[1, t]),
+                    copy(cross_ref.at[t], low.at[2, t], low_sem.at[2, t]),
+                ]
+            return [
+                copy(own_ref.at[t, mine, :], wide.at[t], wide_sem.at[t]),
+                copy(keep_ref.at[t], low.at[0, t], low_sem.at[0, t]),
+            ]
+
+        for o in order:
+            for c in loads(*o):
+                c.start()
+        waits = []
+        for side, t in order:
+            for c in loads(side, t):
+                c.wait()
+            if side:
+                out_buf[1, t] = low[1, t].astype(F32) + low[2, t].astype(F32)
+            else:
+                out_buf[0, t] = wide[t] + low[0, t].astype(F32)
+            target = (dk, dv)[t].at[:, (1 - core if side else core) * MINE + head, 0, :]
+            waits.append(copy(out_buf.at[side, t], target, out_sem.at[side, t]))
+            waits[-1].start()
+        for w in waits:
+            w.wait()
+
+    return pl.pallas_call(
+        body,
+        in_specs=[SCALAR] + [HBM] * 6,
+        out_specs=[HBM] * 2,
+        out_shape=[like(key_grad.shape, F32)] * 2,
+        scratch_shapes=[
+            pltpu.VMEM((2, tokens, width), F32),
+            pltpu.VMEM((3, 2, tokens, width), BF16),
+            pltpu.VMEM((2, 2, tokens, width), F32),
+            pltpu.SemaphoreType.DMA((2,)),
+            pltpu.SemaphoreType.DMA((3, 2)),
+            pltpu.SemaphoreType.DMA((2, 2)),
+        ],
+        input_output_aliases={5: 0, 6: 1},
+        compiler_params=PARAMS,
+        cost_estimate=cost(tokens * width * 36),
+        name="finish_last",
+    )(place, own, got_own, back_keep, back_cross, key_grad, value_grad)
 
 
 def terms(query_tensor, key_tensor, value_tensor, output_gradient, logsumexp, row_inner_products):
@@ -403,19 +472,18 @@
     for c, size in enumerate(GROUPS):
         for slot in range(size):
             h = len(own)
-            mine, theirs, query_grad, sent_dq = attend(h, slot, *shared, *far[c], query_grad, sent_dq)
+            mine, *theirs, query_grad, sent_dq = attend(h, slot, *shared, *far[c], query_grad, sent_dq, h == MINE - 1)
             own.append(mine)
-            back.append(rotated(theirs, -2))
+            back.append(rotated(theirs[0], -2))
+    back_cross = crossed(theirs[1], -2)
     got_dq = partner(sent_dq)
     (query_grad,) = write(range(MINE), 2, place, got_dq, [query_grad])
+    got_own = partner(theirs[2])
     early = range(MINE - 1)
     key_grad, value_grad, send = finish(early, place, own[:-1], back[:-1], None, None)
     got = partner(send)
     key_grad, value_grad = write(early, 1, place, got, [key_grad, value_grad])
-    last = [MINE - 1]
-    key_grad, value_grad, send = finish(last, place, own[-1:], back[-1:], key_grad, value_grad)
-    got = partner(send)
-    key_grad, value_grad = write(last, 1, place, got, [key_grad, value_grad])
+    key_grad, value_grad = finish_last(MINE - 1, place, own[-1], got_own, back[-1], back_cross, key_grad, value_grad)
     return (
         query_grad.reshape(tokens, qheads, width),
         key_grad.reshape(tokens, kheads, width),

time: 140 us -> 127 us (0.907)
  waiting for transfers between devices: 53.4 us -> 41 us
    ppermute x8, waiting for transfers between devices: 48 us -> 31.5 us  [rotated(): return lax.ppermute(x, 'seq', [(i, (i + by) % count) for i in range(count)])]
    ppermute x4 -> x5, waiting for transfers between devices: 5.37 us -> 9.51 us  [crossed(): lax.ppermute(x, 'seq', [(i, (i + by) % count ^ 1) for i in range(count)])]
    pallas_call x4 -> x5, Pallas kernels: 37.7 us -> 39.9 us  [the longest x4 37.7 us: attend(): pl.pallas_call(body, in_specs=in_specs, out_specs=[HBM] * (6 if split els...]
    pallas_call x2 -> x1, Pallas kernels: 6.71 us -> 4.65 us  [finish(): pl.pallas_call(body, in_specs=in_specs, out_specs=[HBM] * 3, out_shape=[l...]
    ppermute x4 -> x5, starting transfers between devices: 2 us -> 3.92 us  [crossed(): lax.ppermute(x, 'seq', [(i, (i + by) % count ^ 1) for i in range(count)])]
    pallas_call x3 -> x2, Pallas kernels: 3.66 us -> 2.8 us  [write(): pl.pallas_call(body, in_specs=[SCALAR, HBM] + [HBM] * len(outs), out_spec...]
  transfers between devices with their start and end apart: 18 -> 19, of which waited for: 7 -> 6; matrix products, arithmetic and copies ran while one was open for 0% -> 0% of each run, Pallas kernels for 33% -> 42%
where the time goes in v1:
time: 127 us; the launch traced here: 126 us
  Pallas kernels  59.2 us (47%)
  waiting for transfers between devices  41 us (32%)
  starting transfers between devices  22.7 us (18%)
  local copies, waits for them, and re-layouts  1.6 us (1%)
    pallas_call x4, Pallas kernels, attend(): pl.pallas_call(body, in_specs=in_specs, out_specs=[HBM] * (6 if split els...  37.7 us
    ppermute x8, waiting for transfers between devices, rotated(): return lax.ppermute(x, 'seq', [(i, (i + by) % count) for i in range(count)])  31.5 us
    ppermute x8, starting transfers between devices, rotated(): return lax.ppermute(x, 'seq', [(i, (i + by) % count) for i in range(count)])  17.3 us
    ppermute x5, waiting for transfers between devices, crossed(): lax.ppermute(x, 'seq', [(i, (i + by) % count ^ 1) for i in range(count)])  9.51 us
    pallas_call x2, Pallas kernels, pack_qg(): pl.pallas_call(body, in_specs=[SCALAR, GIVEN, GIVEN], out_specs=HBM, out_...  7.51 us
    pallas_call x1, Pallas kernels, finish(): pl.pallas_call(body, in_specs=in_specs, out_specs=[HBM] * 3, out_shape=[l...  4.65 us
    pallas_call x1, Pallas kernels, pack_kv(): pl.pallas_call(body, in_specs=[SCALAR] + [GIVEN] * 4, out_specs=[HBM] * (...  4.36 us
    ppermute x5, starting transfers between devices, crossed(): lax.ppermute(x, 'seq', [(i, (i + by) % count ^ 1) for i in range(count)])  3.92 us
  transfers between devices with their start and end apart: 19, of which 6 were waited for; matrix products, arithmetic and copies ran while one was open for 0% of the time, Pallas kernels for 42%

profile of v1, /device:TPU:6, one launch (start us, length us, event | category | flops | bytes accessed | tf_op | source)
XLA Modules:
  0.0 125.5 jit_solution(17931520477513751654)
XLA Ops:
  0.6 3.7 %pack_qg.3 = bf16[4,2,2,512,128]{4,3,2,1,0:T(8,128)(2,1)} custom-call(s32[1]{0:T(128)} %bitcast.place_ref, f32[512,16,1,128]{3,2,1,0:T(1,128)} %bitcast.8, f32[512,16,1,128]{3,2,1,0:T(1,128)} %bitcast.10), custom_call_target="tpu_custom_call" | custom-call | bytes 6291456 | tf_op jit(solution)/shard_map/pack_qg/pallas_call | solution.py:144
  4.4 0.1 collective-permute-start
  4.5 4.4 %pack_kv.1 = (bf16[4,2,512,128]{3,2,1,0:T(8,128)(2,1)}, bf16[1,2,512,128]{3,2,1,0:T(8,128)(2,1)}, bf16[1,2,512,128]{3,2,1,0:T(8,128)(2,1)}, bf16[1,2,512,128]{3,...) custom-call(s32[1]{0:T(128)} %bitcast.place_ref, ...), custom_call_target="tpu_custom_call" | custom-call | bytes 6291456 | tf_op jit(solution)/shard_map/pack_kv/pallas_call | solution.py:92
  8.8 0.6 collective-permute-start.2
  9.4 1.3 %collective-permute-start.10 = (bf16[1,2,512,128]{3,2,1,0:T(8,128)(2,1)}, bf16[1,2,512,128]{3,2,1,0:T(8,128)(2,1)S(1)}, u32[]{:S(2)}, u32[]{:S(2)}) collective-permute-start(bf16[1,2,512,128]{3,2,1,0:T(8,128)(2,1)} %get-tuple-element.49), channel_id=1, source_target_pairs={{0,6},{2,4},{4,10},{6,8},{8,14},{10,12},{12,18},{14,16},{16,22},{1... | collective-permute-start | bytes 786440 | tf_op jit(solution)/shard_map/ppermute | solution.py:38
  10.7 1.6 %collective-permute-start.9 = (bf16[1,2,512,128]{3,2,1,0:T(8,128)(2,1)}, bf16[1,2,512,128]{3,2,1,0:T(8,128)(2,1)}, u32[]{:S(2)}, u32[]{:S(2)}) collective-permute-start(bf16[1,2,512,128]{3,2,1,0:T(8,128)(2,1)} %get-tuple-element.48), channel_id=1, source_target_pairs={{0,4},{2,6},{4,8},{6,10},{8,12},{10,14},{12,16},{14,18},{16,20},{1... | collective-permute-start | bytes 786440 | tf_op jit(solution)/shard_map/ppermute | solution.py:33
  12.2 0.1 collective-permute-start.1
  12.4 3.8 %pack_qg.2.qm = bf16[4,2,2,512,128]{4,3,2,1,0:T(8,128)(2,1)} custom-call(s32[1]{0:T(128)} %bitcast.place_ref, f32[512,16,1,128]{3,2,1,0:T(1,128)} %bitcast.9, f32[512,16,1,128]{3,2,1,0:T(1,128)} %bitcast.11), custom_call_target="tpu_custom_call" | custom-call | bytes 6291456 | tf_op jit(solution)/shard_map/pack_qg/pallas_call | solution.py:144
  16.2 1.4 %collective-permute-start.7 = (bf16[1,2,512,128]{3,2,1,0:T(8,128)(2,1)}, bf16[1,2,512,128]{3,2,1,0:T(8,128)(2,1)S(1)}, u32[]{:S(2)}, u32[]{:S(2)}) collective-permute-start(bf16[1,2,512,128]{3,2,1,0:T(8,128)(2,1)} %get-tuple-element.46), channel_id=1, source_target_pairs={{0,4},{2,6},{4,8},{6,10},{8,12},{10,14},{12,16},{14,18},{16,20},{1... | collective-permute-start | bytes 786440 | tf_op jit(solution)/shard_map/ppermute | solution.py:33
  17.5 4.8 %collective-permute-done.10.ft = bf16[1,2,512,128]{3,2,1,0:T(8,128)(2,1)S(1)} collective-permute-done((bf16[1,2,512,128]{3,2,1,0:T(8,128)(2,1)}, bf16[1,2,512,128]{3,2,1,0:T(8,128)(2,1)S(1)}, u32[]{:S(2)}, u32[]{:S(2)}) %collective-permute-start.10) | collective-permute-done | bytes 262176 | tf_op jit(solution)/shard_map/ppermute | solution.py:38
  22.3 6.9 %collective-permute-done.9.fm = bf16[1,2,512,128]{3,2,1,0:T(8,128)(2,1)} collective-permute-done((bf16[1,2,512,128]{3,2,1,0:T(8,128)(2,1)}, bf16[1,2,512,128]{3,2,1,0:T(8,128)(2,1)}, u32[]{:S(2)}, u32[]{:S(2)}) %collective-permute-start.9) | collective-permute-done | bytes 262176 | tf_op jit(solution)/shard_map/ppermute | solution.py:33
  29.4 1.6 %copy-done = bf16[4,2,2,512,128]{4,3,2,1,0:T(8,128)(2,1)S(1)} copy-done((bf16[4,2,2,512,128]{4,3,2,1,0:T(8,128)(2,1)S(1)}, bf16[4,2,2,512,128]{4,3,2,1,0:T(8,128)(2,1)}, u32[]{:S(2)}) %copy-start) | copy-done | bytes 2097176
  31.0 9.5 %attend.4 = (f32[2,1024,128]{2,1,0:T(8,128)S(1)}, bf16[2,1024,128]{2,1,0:T(8,128)(2,1)S(1)}, f32[512,16,1,128]{3,2,1,0:T(1,128)}, bf16[4,2,512,128]{3,2,1,0:T(8,128)(2,1)S(1)}) custom-call(s32[1]{0:T(128)} %bitcast.place_ref, bf16[4,2,2,512,128]{4,3,2,1,0:T(8,128)(2,1)S(1)} %copy-done, bf16[4,2,2,512,128]{4,3,2,1,0:T(8,128)(2,1)} %collective-permute-done.qt, ...), custom_call_target="tpu_custom_call" | custom-call | flops 3355443200 | bytes 2621440 | tf_op jit(solution)/shard_map/attend/pallas_call | solution.py:258
  40.5 2.6 %collective-permute-start.4 = (bf16[1,2,512,128]{3,2,1,0:T(8,128)(2,1)S(1)}, bf16[1,2,512,128]{3,2,1,0:T(8,128)(2,1)S(1)}, u32[]{:S(2)}, u32[]{:S(2)}) collective-permute-start(bf16[1,2,512,128]{3,2,1,0:T(8,128)(2,1)S(1)} %copy-done.3), channel_id=1, source_target_pairs={{0,6},{2,4},{4,10},{6,8},{8,14},{10,12},{12,18},{14,16},{16,22},{1... | collective-permute-start | bytes 786440 | tf_op jit(solution)/shard_map/ppermute | solution.py:38
  43.1 9.4 %attend.5 = (f32[2,1024,128]{2,1,0:T(8,128)S(1)}, bf16[2,1024,128]{2,1,0:T(8,128)(2,1)S(1)}, f32[512,16,1,128]{3,2,1,0:T(1,128)}, bf16[4,2,512,128]{3,2,1,0:T(8,128)(2,1)S(1)}) custom-call(s32[1]{0:T(128)} %bitcast.place_ref, bf16[4,2,2,512,128]{4,3,2,1,0:T(8,128)(2,1)S(1)} %copy-done, ...), custom_call_target="tpu_custom_call", output_to_operand_aliasing={{2}: (9, {}), {3}: (10, {})} | custom-call | flops 3355443200 | bytes 2621440 | tf_op jit(solution)/shard_map/attend/pallas_call | solution.py:258
  52.5 9.4 %attend.6 = (f32[2,1024,128]{2,1,0:T(8,128)S(1)}, bf16[2,1024,128]{2,1,0:T(8,128)(2,1)S(1)}, f32[512,16,1,128]{3,2,1,0:T(1,128)}, bf16[4,2,512,128]{3,2,1,0:T(8,128)(2,1)S(1)}) custom-call(s32[1]{0:T(128)} %bitcast.place_ref, bf16[4,2,2,512,128]{4,3,2,1,0:T(8,128)(2,1)S(1)} %copy-done, ...), custom_call_target="tpu_custom_call", output_to_operand_aliasing={{2}: (9, {}), {3}: (10, {})} | custom-call | flops 3355443200 | bytes 2621440 | tf_op jit(solution)/shard_map/attend/pallas_call | solution.py:258
  62.0 4.0 %collective-permute-start.17 = (bf16[2,1024,128]{2,1,0:T(8,128)(2,1)S(1)}, bf16[2,1024,128]{2,1,0:T(8,128)(2,1)S(1)}, u32[]{:S(2)}, u32[]{:S(2)}) collective-permute-start(bf16[2,1024,128]{2,1,0:T(8,128)(2,1)S(1)} %get-tuple-element.67), channel_id=1, source_target_pairs={{0,124},{2,126},{4,0},{6,2},{8,4},{10,6},{12,8},{14,10},{16,12},{1... | collective-permute-start | bytes 1572872 | tf_op jit(solution)/shard_map/ppermute | solution.py:33
  65.9 2.0 %collective-permute-start.16 = (bf16[2,1024,128]{2,1,0:T(8,128)(2,1)S(1)}, bf16[2,1024,128]{2,1,0:T(8,128)(2,1)S(1)}, u32[]{:S(2)}, u32[]{:S(2)}) collective-permute-start(bf16[2,1024,128]{2,1,0:T(8,128)(2,1)S(1)} %get-tuple-element.66), channel_id=1, source_target_pairs={{0,124},{2,126},{4,0},{6,2},{8,4},{10,6},{12,8},{14,10},{16,12},{1... | collective-permute-start | bytes 1572872 | tf_op jit(solution)/shard_map/ppermute | solution.py:33
  67.9 1.6 %collective-permute-start.15 = (bf16[2,1024,128]{2,1,0:T(8,128)(2,1)S(1)}, bf16[2,1024,128]{2,1,0:T(8,128)(2,1)S(1)}, u32[]{:S(2)}, u32[]{:S(2)}) collective-permute-start(bf16[2,1024,128]{2,1,0:T(8,128)(2,1)S(1)} %get-tuple-element.65), channel_id=1, source_target_pairs={{0,124},{2,126},{4,0},{6,2},{8,4},{10,6},{12,8},{14,10},{16,12},{1... | collective-permute-start | bytes 1572872 | tf_op jit(solution)/shard_map/ppermute | solution.py:33
  69.6 9.4 %attend.7 = (f32[2,1024,128]{2,1,0:T(8,128)S(1)}, bf16[2,512,128]{2,1,0:T(8,128)(2,1)S(1)}, bf16[2,512,128]{2,1,0:T(8,128)(2,1)S(1)}, bf16[2,512,128]{2,1,0:T(8,...) custom-call(s32[1]{0:T(128)} %bitcast.place_ref, ...), custom_call_target="tpu_custom_call", output_to_operand_aliasing={{4}: (9, {}), {5}: (10, {})} | custom-call | flops 3355443200 | bytes 2621440 | tf_op jit(solution)/shard_map/attend/pallas_call | solution.py:258
  79.0 0.1 collective-permute-start.11
  79.1 10.4 %collective-permute-done.16.rest_4_ = bf16[2,1024,128]{2,1,0:T(8,128)(2,1)S(1)} collective-permute-done((bf16[2,1024,128]{2,1,0:T(8,128)(2,1)S(1)}, bf16[2,1024,128]{2,1,0:T(8,128)(2,1)S(1)}, u32[]{:S(2)}, u32[]{:S(2)}) %collective-permute-start.16) | collective-permute-done | bytes 524320 | tf_op jit(solution)/shard_map/ppermute | solution.py:33
  89.5 10.3 %collective-permute-done.15.rest_3_ = bf16[2,1024,128]{2,1,0:T(8,128)(2,1)S(1)} collective-permute-done((bf16[2,1024,128]{2,1,0:T(8,128)(2,1)S(1)}, bf16[2,1024,128]{2,1,0:T(8,128)(2,1)S(1)}, u32[]{:S(2)}, u32[]{:S(2)}) %collective-permute-start.15) | collective-permute-done | bytes 524320 | tf_op jit(solution)/shard_map/ppermute | solution.py:33
  99.8 4.7 %finish.1 = (f32[512,8,1,128]{3,2,1,0:T(1,128)}, f32[512,8,1,128]{3,2,1,0:T(1,128)}, bf16[3,2,512,128]{3,2,1,0:T(8,128)(2,1)S(1)}) custom-call(s32[1]{0:T(128)} %bitcast.place_ref, f32[2,1024,128]{2,1,0:T(8,128)S(1)} %get-tuple-element.62.rest_0_, f32[2,1024,128]{2,1,0:T(8,128)S(1)} %get-tuple-element.63.rest_1_, ...), custom_call_target="tpu_custom_call" | custom-call | bytes 7077888 | tf_op jit(solution)/shard_map/finish/pallas_call | solution.py:334
  104.5 0.1 collective-permute-start.18
  104.6 0.5 collective-permute-start.12
  105.1 6.7 %collective-permute-start.13 = (bf16[2,512,128]{2,1,0:T(8,128)(2,1)S(1)}, bf16[2,512,128]{2,1,0:T(8,128)(2,1)S(1)}, u32[]{:S(2)}, u32[]{:S(2)}) collective-permute-start(bf16[2,512,128]{2,1,0:T(8,128)(2,1)S(1)} %get-tuple-element.60), channel_id=1, source_target_pairs={{0,124},{2,126},{4,0},{6,2},{8,4},{10,6},{12,8},{14,10},{16,12},{1... | collective-permute-start | bytes 786440 | tf_op jit(solution)/shard_map/ppermute | solution.py:33
  111.8 1.5 %write.2 = f32[512,16,1,128]{3,2,1,0:T(1,128)} custom-call(s32[1]{0:T(128)} %bitcast.place_ref, bf16[4,2,512,128]{3,2,1,0:T(8,128)(2,1)S(1)} %collective-permute-done.11.src, f32[512,16,1,128]{3,2,1,0:T(1,128)} %get-tuple-element.57.rest_0_), custom_call_target="tpu_custom_call", output_to_operand_aliasing={{}: (2, {})} | custom-call | bytes 3145728 | tf_op jit(solution)/shard_map/write/pallas_call | solution.py:376
  113.3 1.3 %write.3 = (f32[512,8,1,128]{3,2,1,0:T(1,128)}, f32[512,8,1,128]{3,2,1,0:T(1,128)}) custom-call(s32[1]{0:T(128)} %bitcast.place_ref, bf16[3,2,512,128]{3,2,1,0:T(8,128)(2,1)S(1)} %collective-permute-done.18.src, f32[512,8,1,128]{3,2,1,0:T(1,128)} %get-tuple-element.69.rest_0_, ...), custom_call_target="tpu_custom_call", output_to_operand_aliasing={{0}: (2, {}), {1}: (3, {})} | custom-call | bytes 2359296 | tf_op jit(solution)/shard_map/write/pallas_call | solution.py:376
  114.6 3.9 %collective-permute-done.13.keep_ref = bf16[2,512,128]{2,1,0:T(8,128)(2,1)S(1)} collective-permute-done((bf16[2,512,128]{2,1,0:T(8,128)(2,1)S(1)}, bf16[2,512,128]{2,1,0:T(8,128)(2,1)S(1)}, u32[]{:S(2)}, u32[]{:S(2)}) %collective-permute-start.13) | collective-permute-done | bytes 262176 | tf_op jit(solution)/shard_map/ppermute | solution.py:33
  118.5 4.7 %collective-permute-done.14.cross_ref = bf16[2,512,128]{2,1,0:T(8,128)(2,1)S(1)} collective-permute-done((bf16[2,512,128]{2,1,0:T(8,128)(2,1)S(1)}, bf16[2,512,128]{2,1,0:T(8,128)(2,1)S(1)}, u32[]{:S(2)}, u32[]{:S(2)}) %collective-permute-start.14) | collective-permute-done | bytes 262176 | tf_op jit(solution)/shard_map/ppermute | solution.py:38
  123.2 2.1 %finish_last.1 = (f32[512,8,1,128]{3,2,1,0:T(1,128)}, f32[512,8,1,128]{3,2,1,0:T(1,128)}) custom-call(s32[1]{0:T(128)} %bitcast.place_ref, f32[2,1024,128]{2,1,0:T(8,128)S(1)} %get-tuple-element.58.own_ref, bf16[2,512,128]{2,1,0:T(8,128)(2,1)S(1)} %collective-permute-done.12.got_ref, ...), custom_call_target="tpu_custom_call", output_to_operand_aliasing={{0}: (5, {}), {1}: (6, {})} | custom-call | bytes 2359296 | tf_op jit(solution)/shard_map/finish_last/pallas_call | solution.py:432
  (25 shorter events, 0.1 us)
Async XLA Ops:
  4.4 24.9 %collective-permute-start = (bf16[4,2,2,512,128]{4,3,2,1,0:T(8,128)(2,1)}, bf16[4,2,2,512,128]{4,3,2,1,0:T(8,128)(2,1)}, u32[]{:S(2)}, u32[]{:S(2)}) collective-permute-start(bf16[4,2,2,512,128]{4,3,2,1,0:T(8,128)(2,1)} %pack_qg.3), channel_id=1, source_target_pairs={{0,2},{2,0},{4,6},{6,4},{8,10},{10,8},{12,14},{14,12},{16,18},{18,... | collective-permute-start | bytes 6291464 | tf_op jit(solution)/shard_map/ppermute | solution.py:43
  8.8 20.4 %collective-permute-start.2 = (bf16[4,2,512,128]{3,2,1,0:T(8,128)(2,1)}, bf16[4,2,512,128]{3,2,1,0:T(8,128)(2,1)}, u32[]{:S(2)}, u32[]{:S(2)}) collective-permute-start(bf16[4,2,512,128]{3,2,1,0:T(8,128)(2,1)} %get-tuple-element.41), channel_id=1, source_target_pairs={{0,2},{2,0},{4,6},{6,4},{8,10},{10,8},{12,14},{14,12},{16,18},{18,... | collective-permute-start | bytes 3145736 | tf_op jit(solution)/shard_map/ppermute | solution.py:43
  9.4 12.9 %collective-permute-start.10 = (bf16[1,2,512,128]{3,2,1,0:T(8,128)(2,1)}, bf16[1,2,512,128]{3,2,1,0:T(8,128)(2,1)S(1)}, u32[]{:S(2)}, u32[]{:S(2)}) collective-permute-start(bf16[1,2,512,128]{3,2,1,0:T(8,128)(2,1)} %get-tuple-element.49), channel_id=1, source_target_pairs={{0,6},{2,4},{4,10},{6,8},{8,14},{10,12},{12,18},{14,16},{16,22},{1... | collective-permute-start | bytes 786440 | tf_op jit(solution)/shard_map/ppermute | solution.py:38
  10.7 18.6 %collective-permute-start.9 = (bf16[1,2,512,128]{3,2,1,0:T(8,128)(2,1)}, bf16[1,2,512,128]{3,2,1,0:T(8,128)(2,1)}, u32[]{:S(2)}, u32[]{:S(2)}) collective-permute-start(bf16[1,2,512,128]{3,2,1,0:T(8,128)(2,1)} %get-tuple-element.48), channel_id=1, source_target_pairs={{0,4},{2,6},{4,8},{6,10},{8,12},{10,14},{12,16},{14,18},{16,20},{1... | collective-permute-start | bytes 786440 | tf_op jit(solution)/shard_map/ppermute | solution.py:33
  12.2 17.1 %copy-start.1 = (bf16[4,2,512,128]{3,2,1,0:T(8,128)(2,1)S(1)}, bf16[4,2,512,128]{3,2,1,0:T(8,128)(2,1)}, u32[]{:S(2)}) copy-start(bf16[4,2,512,128]{3,2,1,0:T(8,128)(2,1)} %get-tuple-element.40.km) | copy-start | bytes 3145732
  12.2 17.1 %copy-start.2 = (f32[2,16,512]{2,1,0:T(8,128)S(1)}, f32[2,16,512]{2,1,0:T(8,128)}, u32[]{:S(2)}) copy-start(f32[2,16,512]{2,1,0:T(8,128)} %get-tuple-element.39.rm) | copy-start | bytes 196612
  12.2 3.9 %collective-permute-start.1 = (f32[2,16,512]{2,1,0:T(8,128)}, f32[2,16,512]{2,1,0:T(8,128)S(1)}, u32[]{:S(2)}, u32[]{:S(2)}) collective-permute-start(f32[2,16,512]{2,1,0:T(8,128)} %get-tuple-element.39.rm), channel_id=1, source_target_pairs={{0,2},{2,0},{4,6},{6,4},{8,10},{10,8},{12,14},{14,12},{16,18},{18,... | collective-permute-start | bytes 196616 | tf_op jit(solution)/shard_map/ppermute | solution.py:43
  16.2 24.2 %collective-permute-start.7 = (bf16[1,2,512,128]{3,2,1,0:T(8,128)(2,1)}, bf16[1,2,512,128]{3,2,1,0:T(8,128)(2,1)S(1)}, u32[]{:S(2)}, u32[]{:S(2)}) collective-permute-start(bf16[1,2,512,128]{3,2,1,0:T(8,128)(2,1)} %get-tuple-element.46), channel_id=1, source_target_pairs={{0,4},{2,6},{4,8},{6,10},{8,12},{10,14},{12,16},{14,18},{16,20},{1... | collective-permute-start | bytes 786440 | tf_op jit(solution)/shard_map/ppermute | solution.py:33
  22.3 20.8 %collective-permute-start.8 = (bf16[1,2,512,128]{3,2,1,0:T(8,128)(2,1)}, bf16[1,2,512,128]{3,2,1,0:T(8,128)(2,1)S(1)}, u32[]{:S(2)}, u32[]{:S(2)}) collective-permute-start(bf16[1,2,512,128]{3,2,1,0:T(8,128)(2,1)} %get-tuple-element.47), channel_id=1, source_target_pairs={{0,6},{2,4},{4,10},{6,8},{8,14},{10,12},{12,18},{14,16},{16,22},{1... | collective-permute-start | bytes 786440 | tf_op jit(solution)/shard_map/ppermute | solution.py:38
  29.2 23.3 %collective-permute-start.5 = (bf16[1,2,512,128]{3,2,1,0:T(8,128)(2,1)}, bf16[1,2,512,128]{3,2,1,0:T(8,128)(2,1)S(1)}, u32[]{:S(2)}, u32[]{:S(2)}) collective-permute-start(bf16[1,2,512,128]{3,2,1,0:T(8,128)(2,1)} %get-tuple-element.44), channel_id=1, source_target_pairs={{0,4},{2,6},{4,8},{6,10},{8,12},{10,14},{12,16},{14,18},{16,20},{1... | collective-permute-start | bytes 786440 | tf_op jit(solution)/shard_map/ppermute | solution.py:33
  29.2 23.3 %collective-permute-start.6 = (bf16[1,2,512,128]{3,2,1,0:T(8,128)(2,1)}, bf16[1,2,512,128]{3,2,1,0:T(8,128)(2,1)S(1)}, u32[]{:S(2)}, u32[]{:S(2)}) collective-permute-start(bf16[1,2,512,128]{3,2,1,0:T(8,128)(2,1)} %get-tuple-element.45), channel_id=1, source_target_pairs={{0,6},{2,4},{4,10},{6,8},{8,14},{10,12},{12,18},{14,16},{16,22},{1... | collective-permute-start | bytes 786440 | tf_op jit(solution)/shard_map/ppermute | solution.py:38
  29.3 40.3 %collective-permute-start.3 = (bf16[1,2,512,128]{3,2,1,0:T(8,128)(2,1)}, bf16[1,2,512,128]{3,2,1,0:T(8,128)(2,1)S(1)}, u32[]{:S(2)}, u32[]{:S(2)}) collective-permute-start(bf16[1,2,512,128]{3,2,1,0:T(8,128)(2,1)} %get-tuple-element.42), channel_id=1, source_target_pairs={{0,4},{2,6},{4,8},{6,10},{8,12},{10,14},{12,16},{14,18},{16,20},{1... | collective-permute-start | bytes 786440 | tf_op jit(solution)/shard_map/ppermute | solution.py:33
  29.4 1.6 %copy-start = (bf16[4,2,2,512,128]{4,3,2,1,0:T(8,128)(2,1)S(1)}, bf16[4,2,2,512,128]{4,3,2,1,0:T(8,128)(2,1)}, u32[]{:S(2)}) copy-start(bf16[4,2,2,512,128]{4,3,2,1,0:T(8,128)(2,1)} %pack_qg.2.qm) | copy-start | bytes 6291460
  31.0 9.5 %copy-start.3 = (bf16[1,2,512,128]{3,2,1,0:T(8,128)(2,1)S(1)}, bf16[1,2,512,128]{3,2,1,0:T(8,128)(2,1)}, u32[]{:S(2)}) copy-start(bf16[1,2,512,128]{3,2,1,0:T(8,128)(2,1)} %get-tuple-element.43) | copy-start | bytes 786436
  40.5 29.1 %collective-permute-start.4 = (bf16[1,2,512,128]{3,2,1,0:T(8,128)(2,1)S(1)}, bf16[1,2,512,128]{3,2,1,0:T(8,128)(2,1)S(1)}, u32[]{:S(2)}, u32[]{:S(2)}) collective-permute-start(bf16[1,2,512,128]{3,2,1,0:T(8,128)(2,1)S(1)} %copy-done.3), channel_id=1, source_target_pairs={{0,6},{2,4},{4,10},{6,8},{8,14},{10,12},{12,18},{14,16},{16,22},{1... | collective-permute-start | bytes 786440 | tf_op jit(solution)/shard_map/ppermute | solution.py:38
  62.0 17.1 %collective-permute-start.17 = (bf16[2,1024,128]{2,1,0:T(8,128)(2,1)S(1)}, bf16[2,1024,128]{2,1,0:T(8,128)(2,1)S(1)}, u32[]{:S(2)}, u32[]{:S(2)}) collective-permute-start(bf16[2,1024,128]{2,1,0:T(8,128)(2,1)S(1)} %get-tuple-element.67), channel_id=1, source_target_pairs={{0,124},{2,126},{4,0},{6,2},{8,4},{10,6},{12,8},{14,10},{16,12},{1... | collective-permute-start | bytes 1572872 | tf_op jit(solution)/shard_map/ppermute | solution.py:33
  65.9 23.6 %collective-permute-start.16 = (bf16[2,1024,128]{2,1,0:T(8,128)(2,1)S(1)}, bf16[2,1024,128]{2,1,0:T(8,128)(2,1)S(1)}, u32[]{:S(2)}, u32[]{:S(2)}) collective-permute-start(bf16[2,1024,128]{2,1,0:T(8,128)(2,1)S(1)} %get-tuple-element.66), channel_id=1, source_target_pairs={{0,124},{2,126},{4,0},{6,2},{8,4},{10,6},{12,8},{14,10},{16,12},{1... | collective-permute-start | bytes 1572872 | tf_op jit(solution)/shard_map/ppermute | solution.py:33
  67.9 31.9 %collective-permute-start.15 = (bf16[2,1024,128]{2,1,0:T(8,128)(2,1)S(1)}, bf16[2,1024,128]{2,1,0:T(8,128)(2,1)S(1)}, u32[]{:S(2)}, u32[]{:S(2)}) collective-permute-start(bf16[2,1024,128]{2,1,0:T(8,128)(2,1)S(1)} %get-tuple-element.65), channel_id=1, source_target_pairs={{0,124},{2,126},{4,0},{6,2},{8,4},{10,6},{12,8},{14,10},{16,12},{1... | collective-permute-start | bytes 1572872 | tf_op jit(solution)/shard_map/ppermute | solution.py:33
  79.0 32.8 %collective-permute-start.11 = (bf16[4,2,512,128]{3,2,1,0:T(8,128)(2,1)S(1)}, bf16[4,2,512,128]{3,2,1,0:T(8,128)(2,1)S(1)}, u32[]{:S(2)}, u32[]{:S(2)}) collective-permute-start(bf16[4,2,512,128]{3,2,1,0:T(8,128)(2,1)S(1)} %get-tuple-element.56), channel_id=1, source_target_pairs={{0,2},{2,0},{4,6},{6,4},{8,10},{10,8},{12,14},{14,12},{16,18},{18,... | collective-permute-start | bytes 3145736 | tf_op jit(solution)/shard_map/ppermute | solution.py:43
  104.5 8.8 %collective-permute-start.18 = (bf16[3,2,512,128]{3,2,1,0:T(8,128)(2,1)S(1)}, bf16[3,2,512,128]{3,2,1,0:T(8,128)(2,1)S(1)}, u32[]{:S(2)}, u32[]{:S(2)}) collective-permute-start(bf16[3,2,512,128]{3,2,1,0:T(8,128)(2,1)S(1)} %get-tuple-element.68), channel_id=1, source_target_pairs={{0,2},{2,0},{4,6},{6,4},{8,10},{10,8},{12,14},{14,12},{16,18},{18,... | collective-permute-start | bytes 2359304 | tf_op jit(solution)/shard_map/ppermute | solution.py:43
  104.6 10.0 %collective-permute-start.12 = (bf16[2,512,128]{2,1,0:T(8,128)(2,1)S(1)}, bf16[2,512,128]{2,1,0:T(8,128)(2,1)S(1)}, u32[]{:S(2)}, u32[]{:S(2)}) collective-permute-start(bf16[2,512,128]{2,1,0:T(8,128)(2,1)S(1)} %get-tuple-element.59), channel_id=1, source_target_pairs={{0,2},{2,0},{4,6},{6,4},{8,10},{10,8},{12,14},{14,12},{16,18},{18,... | collective-permute-start | bytes 786440 | tf_op jit(solution)/shard_map/ppermute | solution.py:43
  105.1 13.4 %collective-permute-start.13 = (bf16[2,512,128]{2,1,0:T(8,128)(2,1)S(1)}, bf16[2,512,128]{2,1,0:T(8,128)(2,1)S(1)}, u32[]{:S(2)}, u32[]{:S(2)}) collective-permute-start(bf16[2,512,128]{2,1,0:T(8,128)(2,1)S(1)} %get-tuple-element.60), channel_id=1, source_target_pairs={{0,124},{2,126},{4,0},{6,2},{8,4},{10,6},{12,8},{14,10},{16,12},{1... | collective-permute-start | bytes 786440 | tf_op jit(solution)/shard_map/ppermute | solution.py:33
  111.8 11.4 %collective-permute-start.14 = (bf16[2,512,128]{2,1,0:T(8,128)(2,1)S(1)}, bf16[2,512,128]{2,1,0:T(8,128)(2,1)S(1)}, u32[]{:S(2)}, u32[]{:S(2)}) collective-permute-start(bf16[2,512,128]{2,1,0:T(8,128)(2,1)S(1)} %get-tuple-element.61), channel_id=1, source_target_pairs={{0,126},{2,124},{4,2},{6,0},{8,6},{10,4},{12,10},{14,8},{16,14},{1... | collective-permute-start | bytes 786440 | tf_op jit(solution)/shard_map/ppermute | solution.py:38
